TPU v7x, 512 devices: a whole 4x8x8 slice. The times are simulated.
512 devices in a mesh: grp: 8 (over z_hi, core), shard: 64 (over z_lo, y, x).
Axes of the slice: x: 4, y: 8, z: 8 (z_hi: 4, z_lo: 2; z = z_hi * 2 + z_lo), core: 2. Of those that a mesh axis runs over, the one named last changes fastest.
Arguments:
- gradients: float32 [8, 1024, 512], P('grp', 'shard'), may hold values from -6 to 6
- weight: float32 [1024, 512], P('shard'), may hold values from -0.1875 to 0.1875
- moment: float32 [1024, 512], P('shard'), may hold values from -4 to 4
- second: float32 [1024, 512], P('shard'), may hold values from 0.01 to 0.5
- left_gram: float32 [1024, 1024], P('shard'), may hold values from -3 to 60, as said below
- left_basis: float32 [1024, 1024], P('shard'), may hold values from -0.1 to 1.1, as said below
- right_gram: float32 [512, 512], P('shard'), may hold values from -3 to 60, as said below
- right_basis: float32 [512, 512], P('shard'), may hold values from -0.1 to 1.1, as said below
Outputs:
- weight_new: float32 [1024, 512], P('shard')
- moment_new: float32 [1024, 512], P('shard')
- second_new: float32 [1024, 512], P('shard')
- left_new: float32 [1024, 1024], P('shard')
- left_basis_new: float32 [1024, 1024], P('shard')
- right_new: float32 [512, 512], P('shard')
- right_basis_new: float32 [512, 512], P('shard')
Inputs may be any that keep to these rules, and one draw needn't show every extreme that they name: `left_gram`: symmetric positive definite. `right_gram`: symmetric positive definite. `left_basis`: square and of full rank. `right_basis`: square and of full rank.
All inputs are finite; a program needn't handle non-finite values.
Results may differ from a plain program's by a relative error of at most 0.0015.
The roundings to bfloat16 on the way count: a program that leaves them out, or rounds other values in their place, can miss the bound.
Values may be sent and summed in bfloat16 or wider, within the bound.
No kernel may reach another device: no remote copies, remote signals or barrier semaphores. Data moves between devices by JAX's collectives and lax.ppermute only.
A program may use at most 64 MiB of HBM per device.

v0:
```python
import jax
import jax.numpy as jnp
from jax import lax
from jax.sharding import PartitionSpec as P

NS_ITERS = 2
BETA_ONE = 0.9
BETA_TWO = 0.95
GRAM_DECAY = 0.95
ADAM_EPS = 1e-08
NORM_EPS = 1e-06
STEP_SIZE = 0.02
START_SCALE = 0.75
PRECISE = lax.Precision.HIGHEST


def inner_rows(former, latter):
    return lax.dot_general(
        former, latter, (((0,), (0,)), ((), ())), preferred_element_type=jnp.float32
    )


def outer_rows(former, latter):
    return lax.dot_general(
        former, latter, (((1,), (1,)), ((), ())), preferred_element_type=jnp.float32
    )


def start_rows(power_rows, column_sums):
    scaled = START_SCALE * power_rows / jnp.sqrt(column_sums + NORM_EPS)
    return lax.optimization_barrier(scaled.astype(jnp.bfloat16))


def left_sweep(current):
    segment = lax.all_gather(current, "shard", axis=0, tiled=True)
    square = outer_rows(current, segment).astype(jnp.bfloat16)
    running = jnp.dot(square, segment, preferred_element_type=jnp.float32)
    return 1.5 * current.astype(jnp.float32) - 0.5 * running


def right_sweep(current):
    segment = lax.all_gather(current, "shard", axis=0, tiled=True)
    square = outer_rows(current, segment).astype(jnp.bfloat16)
    running = jnp.dot(square, segment, preferred_element_type=jnp.float32)
    return 1.5 * current.astype(jnp.float32) - 0.5 * running


def local(gradients, weight, moment, second, left_gram, left_basis, right_gram, right_basis):
    local_rows = weight.shape[0]
    right_rows = right_gram.shape[0]
    row_first = lax.axis_index("shard") * local_rows
    right_first = lax.axis_index("shard") * right_rows
    gradient = lax.psum(gradients[0], "grp") / lax.axis_size("grp")
    moment_new = BETA_ONE * moment + (1.0 - BETA_ONE) * gradient
    grad_half = gradient.astype(jnp.bfloat16)
    moment_half = moment_new.astype(jnp.bfloat16)
    left_half = left_basis.astype(jnp.bfloat16)
    right_whole = lax.all_gather(right_basis.astype(jnp.bfloat16), "shard", axis=0, tiled=True)
    right_wide = lax.optimization_barrier(right_whole).astype(jnp.float32)
    basis_part = lax.all_gather(left_half, "shard", axis=0, tiled=True)
    grad_part = lax.all_gather(grad_half, "shard", axis=0, tiled=True)
    basis_columns = lax.dynamic_slice_in_dim(basis_part, row_first, local_rows, 1)
    turned = inner_rows(basis_columns, grad_part)
    gram_block = GRAM_DECAY * left_gram + (1.0 - GRAM_DECAY) * outer_rows(grad_half, grad_part)
    power_rows = jnp.dot(gram_block, basis_part.astype(jnp.float32), precision=PRECISE)
    grad_columns = lax.dynamic_slice_in_dim(grad_part, right_first, right_rows, 1)
    right_terms = inner_rows(grad_columns, grad_part)
    core_state, basis_columns = ((turned, gram_block, power_rows, right_terms), basis_columns)
    core_state, turned_moment = (
        core_state,
        inner_rows(basis_columns, lax.all_gather(moment_half, "shard", axis=0, tiled=True)),
    )
    turned_grad, left_new, left_power, right_terms = core_state
    right_new = GRAM_DECAY * right_gram + (1.0 - GRAM_DECAY) * right_terms
    rotated_grad = jnp.dot(
        turned_grad.astype(jnp.bfloat16), right_whole, preferred_element_type=jnp.float32
    )
    rotated_moment = jnp.dot(
        turned_moment.astype(jnp.bfloat16), right_whole, preferred_element_type=jnp.float32
    )
    second_new = BETA_TWO * second + (1.0 - BETA_TWO) * rotated_grad * rotated_grad
    direction = (rotated_moment / (jnp.sqrt(second_new) + ADAM_EPS)).astype(jnp.bfloat16)
    returned = outer_rows(direction, right_whole).astype(jnp.bfloat16)
    update = jnp.dot(
        left_half,
        lax.all_gather(returned, "shard", axis=0, tiled=True),
        preferred_element_type=jnp.float32,
    )
    weight_new = weight - STEP_SIZE * update
    right_power = jnp.dot(right_new, right_wide, precision=PRECISE)
    left_sums, right_sums = lax.psum(
        (jnp.sum(left_power * left_power, axis=0), jnp.sum(right_power * right_power, axis=0)),
        "shard",
    )
    right_current = start_rows(right_power, right_sums)
    right_result = right_power
    for sweep in range(NS_ITERS):
        right_result = right_sweep(right_current)
        right_current = lax.optimization_barrier(right_result.astype(jnp.bfloat16))
    left_current = start_rows(left_power, left_sums)
    left_result = left_power
    for sweep in range(NS_ITERS):
        left_result = left_sweep(left_current)
        left_current = lax.optimization_barrier(left_result.astype(jnp.bfloat16))
    return (weight_new, moment_new, second_new, left_new, left_result, right_new, right_result)


def solution(mesh):
    return jax.shard_map(
        local,
        mesh=mesh,
        in_specs=(
            P("grp", "shard", None),
            P("shard", None),
            P("shard", None),
            P("shard", None),
            P("shard", None),
            P("shard", None),
            P("shard", None),
            P("shard", None),
        ),
        out_specs=(
            P("shard", None),
            P("shard", None),
            P("shard", None),
            P("shard", None),
            P("shard", None),
            P("shard", None),
            P("shard", None),
        ),
        check_vma=False,
    )
```

profile of v0, /device:TPU:2, one launch (start us, length us, event | category | flops | bytes accessed | tf_op | source)
XLA Modules:
  0.0 1857.0 jit_solution(10023106520451230898)
XLA Ops:
  7.2 36.2 %psum.21 = f32[16,512]{1,0:T(8,128)S(1)} all-reduce(f32[16,512]{1,0:T(8,128)} %bitcast.32), channel_id=1, replica_groups=mesh['grp'=8,'shard'=64] {'grp'}, use_global_device_ids=true, to_apply=%region_0.0 | all-reduce | flops 8192 | bytes 65536 | tf_op jit(solution)/shard_map/psum | solution.py:53
  43.4 1.4 fusion.29
  44.8 0.0 all-gather.7.cloned.1.call-start
  44.9 1.5 convert_element_type.62
  46.4 0.0 all-gather.9.cloned.1.call-start
  46.4 0.7 all-gather.9.cloned.1.call-update
  47.1 0.0 all-gather.15.cloned.1.call-start
  47.1 0.7 convert_element_type.65
  47.9 154.5 %all_gather.29 = bf16[512,512]{1,0:T(8,128)(2,1)S(1)} all-gather(bf16[8,512]{1,0:T(8,128)(2,1)S(1)} %convert_element_type.65), channel_id=1, replica_groups=mesh['grp'=8,'shard'=64] {'shard'}, dimensions={0}, use_global_device_ids=true | all-gather | bytes 532480 | tf_op jit(solution)/shard_map/all_gather | solution.py:58
  202.3 138.1 %all-gather.11.cloned.1.call-done = bf16[1024,512]{1,0:T(8,128)(2,1)} async-done(((bf16[16,512]{1,0:T(8,128)(2,1)}), bf16[1024,512]{1,0:T(8,128)(2,1)}) %all-gather.11.cloned.1.call-update) | async-done | bytes 1048592 | tf_op jit(solution)/shard_map/all_gather | solution.py:61
  340.4 1.7 fusion.8
  342.1 0.3 multiply_reduce_fusion.1
  342.4 1.6 fusion.2
  344.1 298.7 %all-gather.7.cloned.1.call-done = bf16[1024,1024]{1,0:T(8,128)(2,1)} async-done(((bf16[16,1024]{1,0:T(8,128)(2,1)}), bf16[1024,1024]{1,0:T(8,128)(2,1)}) %all-gather.7.cloned.1.call-update) | async-done | bytes 2097168 | tf_op jit(solution)/shard_map/all_gather | solution.py:60
  642.8 2.5 multiply_reduce_fusion
  645.4 156.0 %all-reduce = (f32[1024]{0:T(1024)S(1)}, f32[512]{0:T(512)S(1)}) all-reduce(f32[1024]{0:T(1024)S(1)} %get-tuple-element.12, f32[512]{0:T(512)S(1)} %get-tuple-element.14), channel_id=1, replica_groups=mesh['grp'=8,'shard'=64] {'shard'}, use_global_device_ids=true, to_apply=%region_2.0 | all-reduce | flops 1536 | bytes 12288 | tf_op jit(solution)/shard_map/psum | solution.py:91
  801.3 0.6 divide_convert_fusion
  802.0 0.0 all-gather.13.cloned.1.call-start
  802.1 140.5 %all-gather.9.cloned.1.call-done = bf16[1024,512]{1,0:T(8,128)(2,1)} async-done(((bf16[16,512]{1,0:T(8,128)(2,1)}), bf16[1024,512]{1,0:T(8,128)(2,1)}) %all-gather.9.cloned.1.call-update) | async-done | bytes 1048592 | tf_op jit(solution)/shard_map/all_gather | solution.py:71
  942.6 1.7 convolution_convert_fusion.3
  944.3 1.5 fusion.18
  945.8 1.0 convolution_convert_fusion.4
  946.8 0.0 all-gather.17.cloned.1.call-start
  946.8 298.1 %all-gather.15.cloned.1.call-done = bf16[1024,1024]{1,0:T(8,128)(2,1)} async-done(((bf16[16,1024]{1,0:T(8,128)(2,1)}), bf16[1024,1024]{1,0:T(8,128)(2,1)}) %all-gather.15.cloned.1.call-update) | async-done | bytes 2097168 | tf_op jit(solution)/shard_map/all_gather | solution.py:35
  1244.9 3.8 fusion.3
  1248.8 154.3 %all_gather.34 = bf16[512,512]{1,0:T(8,128)(2,1)S(1)} all-gather(bf16[8,512]{1,0:T(8,128)(2,1)S(1)} %divide_convert_fusion.1), channel_id=1, replica_groups=mesh['grp'=8,'shard'=64] {'shard'}, dimensions={0}, use_global_device_ids=true | all-gather | bytes 532480 | tf_op jit(solution)/shard_map/all_gather | solution.py:42
  1403.1 0.4 fusion.11
  1403.5 157.4 %all_gather.35 = bf16[512,512]{1,0:T(8,128)(2,1)S(1)} all-gather(bf16[8,512]{1,0:T(8,128)(2,1)S(1)} %fusion.11), channel_id=1, replica_groups=mesh['grp'=8,'shard'=64] {'shard'}, dimensions={0}, use_global_device_ids=true | all-gather | bytes 532480 | tf_op jit(solution)/shard_map/all_gather | solution.py:42
  1560.9 1.0 fusion.9
  1561.9 2.1 fusion.5
  1564.0 282.3 %all-gather.17.cloned.1.call-done = bf16[1024,1024]{1,0:T(8,128)(2,1)} async-done(((bf16[16,1024]{1,0:T(8,128)(2,1)}), bf16[1024,1024]{1,0:T(8,128)(2,1)}) %all-gather.17.cloned.1.call-update) | async-done | bytes 2097168 | tf_op jit(solution)/shard_map/all_gather | solution.py:35
  1846.3 3.8 fusion
  (32 shorter events, 0.2 us)
Async XLA Ops:
  7.2 335.3 %copy-start.8 = (f32[16,1024]{1,0:T(8,128)S(1)}, f32[16,1024]{1,0:T(8,128)}, u32[]{:S(2)}) copy-start(f32[16,1024]{1,0:T(8,128)} %param.12) | copy-start | bytes 196612
  7.2 333.2 %all-gather.11.cloned.1.call-start = ((), (), s32[]{:S(2)}) async-start(), calls=%async_computation.2 | async-start | bytes 1064960 | tf_op jit(solution)/shard_map/all_gather | solution.py:61
  44.8 297.6 %copy-start.5 = (bf16[16,512]{1,0:T(8,128)(2,1)S(1)}, bf16[16,512]{1,0:T(8,128)(2,1)}, u32[]{:S(2)}) copy-start(bf16[16,512]{1,0:T(8,128)(2,1)} %get-tuple-element.11) | copy-start | bytes 49156
  44.8 598.0 %all-gather.7.cloned.1.call-start = ((), (), s32[]{:S(2)}) async-start(), calls=%async_computation | async-start | bytes 2129920 | tf_op jit(solution)/shard_map/all_gather | solution.py:60
  46.4 896.2 %all-gather.9.cloned.1.call-start = ((), (), s32[]{:S(2)}) async-start(), calls=%async_computation.1 | async-start | bytes 1064960 | tf_op jit(solution)/shard_map/all_gather | solution.py:71
  47.1 1197.8 %all-gather.15.cloned.1.call-start = ((), (), s32[]{:S(2)}) async-start(), calls=%async_computation.4 | async-start | bytes 2129920 | tf_op jit(solution)/shard_map/all_gather | solution.py:35
  342.1 602.2 %copy-start.7 = (f32[8,512]{1,0:T(8,128)}, f32[8,512]{1,0:T(8,128)S(1)}, u32[]{:S(2)}) copy-start(f32[8,512]{1,0:T(8,128)S(1)} %fusion.8) | copy-start | bytes 49156
  344.0 601.7 %copy-start.4 = (f32[16,1024]{1,0:T(8,128)}, f32[16,1024]{1,0:T(8,128)S(1)}, u32[]{:S(2)}) copy-start(f32[16,1024]{1,0:T(8,128)S(1)} %fusion.2) | copy-start | bytes 196612
  344.0 600.2 %copy-start = (bf16[1024,512]{1,0:T(8,128)(2,1)S(1)}, bf16[1024,512]{1,0:T(8,128)(2,1)}, u32[]{:S(2)}) copy-start(bf16[1024,512]{1,0:T(8,128)(2,1)} %all-gather.11.cloned.1.call-done) | copy-start | bytes 3145732
  344.1 600.2 %copy-start.9 = (f32[16,512]{1,0:T(8,128)S(1)}, f32[16,512]{1,0:T(8,128)}, u32[]{:S(2)}) copy-start(f32[16,512]{1,0:T(8,128)} %param.11) | copy-start | bytes 98308
  802.0 759.9 %all-gather.13.cloned.1.call-start = ((), (), s32[]{:S(2)}) async-start(), calls=%async_computation.3 | async-start | bytes 1064960 | tf_op jit(solution)/shard_map/all_gather | solution.py:86
  802.0 442.9 %copy-start.2 = (bf16[16,1024]{1,0:T(8,128)(2,1)S(1)}, bf16[16,1024]{1,0:T(8,128)(2,1)}, u32[]{:S(2)}) copy-start(bf16[16,1024]{1,0:T(8,128)(2,1)} %divide_convert_fusion) | copy-start | bytes 98308
  945.8 303.0 %copy-start.6 = (f32[16,512]{1,0:T(8,128)}, f32[16,512]{1,0:T(8,128)S(1)}, u32[]{:S(2)}) copy-start(f32[16,512]{1,0:T(8,128)S(1)} %fusion.18) | copy-start | bytes 98308
  946.8 899.6 %all-gather.17.cloned.1.call-start = ((), (), s32[]{:S(2)}) async-start(), calls=%async_computation.5 | async-start | bytes 2129920 | tf_op jit(solution)/shard_map/all_gather | solution.py:35
  1248.7 313.2 %copy-start.3 = (bf16[16,1024]{1,0:T(8,128)(2,1)S(1)}, bf16[16,1024]{1,0:T(8,128)(2,1)}, u32[]{:S(2)}) copy-start(bf16[16,1024]{1,0:T(8,128)(2,1)} %convert_element_type.62) | copy-start | bytes 98308
  1248.7 313.2 %copy-start.10 = (f32[16,512]{1,0:T(8,128)S(1)}, f32[16,512]{1,0:T(8,128)}, u32[]{:S(2)}) copy-start(f32[16,512]{1,0:T(8,128)} %param.9) | copy-start | bytes 98308
  1248.8 597.6 %copy-start.1 = (bf16[16,1024]{1,0:T(8,128)(2,1)S(1)}, bf16[16,1024]{1,0:T(8,128)(2,1)}, u32[]{:S(2)}) copy-start(bf16[16,1024]{1,0:T(8,128)(2,1)} %fusion.3) | copy-start | bytes 98308
Sparse Core Ops, SparseCore 0:
  44.9 295.3 all-gather.10
  343.0 299.7 all-gather.6
  645.5 297.0 all-gather.8
  945.1 299.8 all-gather.14
  1246.9 297.0 all-gather.12
  1546.5 299.7 all-gather.16
where the time goes:
time: 1860 us
  waiting for transfers between devices  1160 us (62%)
  blocking collectives  658 us (35%)
  matrix products  21.4 us (1%)
    all_gather x2, waiting for transfers between devices, left_sweep(): segment = lax.all_gather(current, 'shard', axis=0, tiled=True)  580 us
    all_gather x2, blocking collectives, right_sweep(): segment = lax.all_gather(current, 'shard', axis=0, tiled=True)  312 us
    all_gather x1, waiting for transfers between devices, local(): basis_part = lax.all_gather(left_half, 'shard', axis=0, tiled=True)  299 us
    psum x1, blocking collectives, local(): lax.psum((jnp.sum(left_power * left_power, axis=0), jnp.sum(right_power *...  156 us
    all_gather x1, blocking collectives, local(): lax.all_gather(right_basis.astype(jnp.bfloat16), 'shard', axis=0, tiled=T...  154 us
    all_gather x1, waiting for transfers between devices, local(): lax.all_gather(moment_half, 'shard', axis=0, tiled=True)  141 us
    all_gather x1, waiting for transfers between devices, local(): grad_part = lax.all_gather(grad_half, 'shard', axis=0, tiled=True)  138 us
  transfers between devices with their start and end apart: 6, of which 5 were waited for; matrix products, arithmetic and copies ran while one was open for 1% of the time, Pallas kernels for 0%

commit v1 on v0

--- a/solution.py
+++ b/solution.py
@@ -57,8 +57,13 @@
     left_half = left_basis.astype(jnp.bfloat16)
     right_whole = lax.all_gather(right_basis.astype(jnp.bfloat16), "shard", axis=0, tiled=True)
     right_wide = lax.optimization_barrier(right_whole).astype(jnp.float32)
-    basis_part = lax.all_gather(left_half, "shard", axis=0, tiled=True)
-    grad_part = lax.all_gather(grad_half, "shard", axis=0, tiled=True)
+    basis_part, grad_part = jnp.split(
+        lax.all_gather(
+            jnp.concatenate([left_half, grad_half], axis=1), "shard", axis=0, tiled=True
+        ),
+        [left_half.shape[1]],
+        axis=1,
+    )
     basis_columns = lax.dynamic_slice_in_dim(basis_part, row_first, local_rows, 1)
     turned = inner_rows(basis_columns, grad_part)
     gram_block = GRAM_DECAY * left_gram + (1.0 - GRAM_DECAY) * outer_rows(grad_half, grad_part)

time: 1860 us -> 1560 us (0.84)
  waiting for transfers between devices: 1160 us -> 860 us
    all_gather x2 -> x1, waiting for transfers between devices: 437 us -> 145 us  [local(): lax.all_gather(jnp.concatenate([left_half, grad_half], axis=1), 'shard',...]
  transfers between devices with their start and end apart: 6 -> 5, of which waited for: 5 -> 4; matrix products, arithmetic and copies ran while one was open for 1% -> 1% of each run, Pallas kernels for 0% -> 0%
where the time goes in v1:
time: 1560 us
  waiting for transfers between devices  860 us (55%)
  blocking collectives  659 us (42%)
  matrix products  19.9 us (1%)
    all_gather x2, waiting for transfers between devices, left_sweep(): segment = lax.all_gather(current, 'shard', axis=0, tiled=True)  579 us
    all_gather x2, blocking collectives, right_sweep(): segment = lax.all_gather(current, 'shard', axis=0, tiled=True)  312 us
    psum x1, blocking collectives, local(): lax.psum((jnp.sum(left_power * left_power, axis=0), jnp.sum(right_power *...  156 us
    all_gather x1, blocking collectives, local(): lax.all_gather(right_basis.astype(jnp.bfloat16), 'shard', axis=0, tiled=T...  155 us
    all_gather x1, waiting for transfers between devices, local(): lax.all_gather(jnp.concatenate([left_half, grad_half], axis=1), 'shard',...  145 us
    all_gather x1, waiting for transfers between devices, local(): lax.all_gather(moment_half, 'shard', axis=0, tiled=True)  135 us
    psum x1, blocking collectives, local(): gradient = lax.psum(gradients[0], 'grp') / lax.axis_size('grp')  36.2 us
  transfers between devices with their start and end apart: 5, of which 4 were waited for; matrix products, arithmetic and copies ran while one was open for 1% of the time, Pallas kernels for 0%

profile of v1, /device:TPU:2, one launch (start us, length us, event | category | flops | bytes accessed | tf_op | source)
XLA Modules:
  0.0 1561.2 jit_solution(12477456462300763490)
XLA Ops:
  7.2 36.2 %psum.21 = f32[16,512]{1,0:T(8,128)S(1)} all-reduce(f32[16,512]{1,0:T(8,128)} %bitcast.29), channel_id=1, replica_groups=mesh['grp'=8,'shard'=64] {'grp'}, use_global_device_ids=true, to_apply=%region_0.0 | all-reduce | flops 8192 | bytes 65536 | tf_op jit(solution)/shard_map/psum | solution.py:53
  43.4 0.8 convert_element_type.62
  44.3 1.4 fusion.34
  45.6 0.6 pad_maximum_fusion
  46.3 0.0 all-gather.8.cloned.1.call-start
  46.3 0.7 all-gather.8.cloned.1.call-update
  47.1 0.7 convert_element_type.66
  47.8 154.7 %all_gather.26 = bf16[512,512]{1,0:T(8,128)(2,1)S(1)} all-gather(bf16[8,512]{1,0:T(8,128)(2,1)S(1)} %convert_element_type.66), channel_id=1, replica_groups=mesh['grp'=8,'shard'=64] {'shard'}, dimensions={0}, use_global_device_ids=true | all-gather | bytes 532480 | tf_op jit(solution)/shard_map/all_gather | solution.py:58
  202.5 144.6 %all-gather.6.cloned.1.call-done = bf16[1024,1536]{1,0:T(8,128)(2,1)} async-done(((bf16[16,1536]{1,0:T(8,128)(2,1)}), bf16[1024,1536]{1,0:T(8,128)(2,1)}) %all-gather.6.cloned.1.call-update) | async-done | bytes 3145744 | tf_op jit(solution)/shard_map/all_gather | solution.py:61
  347.1 1.2 slice-done
  348.4 0.4 fusion.8
  348.8 0.3 multiply_reduce_fusion.1
  349.1 1.6 fusion.2
  350.8 0.9 multiply_reduce_fusion
  351.7 156.0 %all-reduce = (f32[1024]{0:T(1024)S(1)}, f32[512]{0:T(512)S(1)}) all-reduce(f32[1024]{0:T(1024)S(1)} %get-tuple-element.12, f32[512]{0:T(512)S(1)} %get-tuple-element.14), channel_id=1, replica_groups=mesh['grp'=8,'shard'=64] {'shard'}, use_global_device_ids=true, to_apply=%region_2.0 | all-reduce | flops 1536 | bytes 12288 | tf_op jit(solution)/shard_map/psum | solution.py:96
  507.7 0.6 divide_convert_fusion
  508.4 0.0 all-gather.10.cloned.1.call-start
  508.5 3.3 split.8
  511.7 135.3 %all-gather.8.cloned.1.call-done = bf16[1024,512]{1,0:T(8,128)(2,1)} async-done(((bf16[16,512]{1,0:T(8,128)(2,1)}), bf16[1024,512]{1,0:T(8,128)(2,1)}) %all-gather.8.cloned.1.call-update) | async-done | bytes 1048592 | tf_op jit(solution)/shard_map/all_gather | solution.py:76
  647.0 1.7 convolution_convert_fusion.3
  648.7 1.7 fusion.18
  650.4 2.2 convolution_convert_fusion.4
  652.6 0.0 all-gather.14.cloned.1.call-start
  652.7 296.9 %all-gather.12.cloned.1.call-done = bf16[1024,1024]{1,0:T(8,128)(2,1)} async-done(((bf16[16,1024]{1,0:T(8,128)(2,1)}), bf16[1024,1024]{1,0:T(8,128)(2,1)}) %all-gather.12.cloned.1.call-update) | async-done | bytes 2097168 | tf_op jit(solution)/shard_map/all_gather | solution.py:35
  949.5 3.8 fusion.3
  953.4 154.4 %all_gather.30 = bf16[512,512]{1,0:T(8,128)(2,1)S(1)} all-gather(bf16[8,512]{1,0:T(8,128)(2,1)S(1)} %divide_convert_fusion.1), channel_id=1, replica_groups=mesh['grp'=8,'shard'=64] {'shard'}, dimensions={0}, use_global_device_ids=true | all-gather | bytes 532480 | tf_op jit(solution)/shard_map/all_gather | solution.py:42
  1107.8 0.4 fusion.11
  1108.1 157.3 %all_gather.31 = bf16[512,512]{1,0:T(8,128)(2,1)S(1)} all-gather(bf16[8,512]{1,0:T(8,128)(2,1)S(1)} %fusion.11), channel_id=1, replica_groups=mesh['grp'=8,'shard'=64] {'shard'}, dimensions={0}, use_global_device_ids=true | all-gather | bytes 532480 | tf_op jit(solution)/shard_map/all_gather | solution.py:42
  1265.4 1.0 fusion.9
  1266.5 2.1 fusion.5
  1268.6 282.4 %all-gather.14.cloned.1.call-done = bf16[1024,1024]{1,0:T(8,128)(2,1)} async-done(((bf16[16,1024]{1,0:T(8,128)(2,1)}), bf16[1024,1024]{1,0:T(8,128)(2,1)}) %all-gather.14.cloned.1.call-update) | async-done | bytes 2097168 | tf_op jit(solution)/shard_map/all_gather | solution.py:35
  1550.9 3.8 fusion
  (35 shorter events, 0.2 us)
Async XLA Ops:
  7.2 340.0 %copy-start.11 = (f32[8,512]{1,0:T(8,128)S(1)}, f32[8,512]{1,0:T(8,128)}, u32[]{:S(2)}) copy-start(f32[8,512]{1,0:T(8,128)} %param.14) | copy-start | bytes 49156
  7.2 339.9 %all-gather.6.cloned.1.call-start = ((), (), s32[]{:S(2)}) async-start(), calls=%async_computation | async-start | bytes 3194880 | tf_op jit(solution)/shard_map/all_gather | solution.py:61
  46.3 600.7 %all-gather.8.cloned.1.call-start = ((), (), s32[]{:S(2)}) async-start(), calls=%async_computation.1 | async-start | bytes 1064960 | tf_op jit(solution)/shard_map/all_gather | solution.py:76
  47.0 902.5 %all-gather.12.cloned.1.call-start = ((), (), s32[]{:S(2)}) async-start(), calls=%async_computation.3 | async-start | bytes 2129920 | tf_op jit(solution)/shard_map/all_gather | solution.py:35
  47.8 301.3 %copy-start.8 = (f32[16,1024]{1,0:T(8,128)S(1)}, f32[16,1024]{1,0:T(8,128)}, u32[]{:S(2)}) copy-start(f32[16,1024]{1,0:T(8,128)} %param.12) | copy-start | bytes 196612
  202.5 148.2 %copy-start.2 = (bf16[512,512]{1,0:T(8,128)(2,1)}, bf16[512,512]{1,0:T(8,128)(2,1)S(1)}, u32[]{:S(2)}) copy-start(bf16[512,512]{1,0:T(8,128)(2,1)S(1)} %all_gather.26) | copy-start | bytes 1572868
  347.1 1.2 slice-start
  347.1 3.6 copy-start
  348.8 163.0 %copy-start.7 = (f32[8,512]{1,0:T(8,128)}, f32[8,512]{1,0:T(8,128)S(1)}, u32[]{:S(2)}) copy-start(f32[8,512]{1,0:T(8,128)S(1)} %fusion.8) | copy-start | bytes 49156
  350.8 161.0 %copy-start.5 = (f32[16,1024]{1,0:T(8,128)}, f32[16,1024]{1,0:T(8,128)S(1)}, u32[]{:S(2)}) copy-start(f32[16,1024]{1,0:T(8,128)S(1)} %fusion.2) | copy-start | bytes 196612
  508.4 758.1 %all-gather.10.cloned.1.call-start = ((), (), s32[]{:S(2)}) async-start(), calls=%async_computation.2 | async-start | bytes 1064960 | tf_op jit(solution)/shard_map/all_gather | solution.py:91
  508.4 140.3 %copy-start.1 = (bf16[1024,1536]{1,0:T(8,128)(2,1)S(1)}, bf16[1024,1536]{1,0:T(8,128)(2,1)}, u32[]{:S(2)}) copy-start(bf16[1024,1536]{1,0:T(8,128)(2,1)} %all-gather.6.cloned.1.call-done) | copy-start | bytes 9437188
  508.5 140.3 %copy-start.9 = (f32[16,512]{1,0:T(8,128)S(1)}, f32[16,512]{1,0:T(8,128)}, u32[]{:S(2)}) copy-start(f32[16,512]{1,0:T(8,128)} %param.11) | copy-start | bytes 98308
  511.7 437.8 %copy-start.4 = (bf16[16,1024]{1,0:T(8,128)(2,1)S(1)}, bf16[16,1024]{1,0:T(8,128)(2,1)}, u32[]{:S(2)}) copy-start(bf16[16,1024]{1,0:T(8,128)(2,1)} %divide_convert_fusion) | copy-start | bytes 98308
  650.4 302.9 %copy-start.6 = (f32[16,512]{1,0:T(8,128)}, f32[16,512]{1,0:T(8,128)S(1)}, u32[]{:S(2)}) copy-start(f32[16,512]{1,0:T(8,128)S(1)} %fusion.18) | copy-start | bytes 98308
  652.6 898.3 %all-gather.14.cloned.1.call-start = ((), (), s32[]{:S(2)}) async-start(), calls=%async_computation.4 | async-start | bytes 2129920 | tf_op jit(solution)/shard_map/all_gather | solution.py:35
  953.3 313.1 %copy-start.10 = (f32[16,512]{1,0:T(8,128)S(1)}, f32[16,512]{1,0:T(8,128)}, u32[]{:S(2)}) copy-start(f32[16,512]{1,0:T(8,128)} %param.9) | copy-start | bytes 98308
  953.4 597.5 %copy-start.3 = (bf16[16,1024]{1,0:T(8,128)(2,1)S(1)}, bf16[16,1024]{1,0:T(8,128)(2,1)}, u32[]{:S(2)}) copy-start(bf16[16,1024]{1,0:T(8,128)(2,1)} %fusion.3) | copy-start | bytes 98308
Sparse Core Ops, SparseCore 0:
  46.4 300.6 all-gather.5
  349.8 297.1 all-gather.7
  649.7 299.8 all-gather.11
  951.5 297.1 all-gather.9
  1251.1 299.7 all-gather.13
